TPU v7x, 256 devices: a whole 4x4x8 slice. The times are simulated.
256 devices in a mesh: box: 64 (over x, z, core), col: 4 (over y).
Axes of the slice: x: 4, y: 4, z: 8, core: 2. Of those that a mesh axis runs over, the one named last changes fastest.
Arguments:
- leaf_maps: float32 [64, 1024, 1024], P('box', None, 'col'), as said below
- leaf_nodes: int32 [64, 4, 256], P('box'), may hold values from 0 to 255, each once within a row
Outputs:
- top_maps: float32 [64, 1024, 1024], P('box', None, 'col')
Inputs may be any that keep to these rules, and one draw needn't show every extreme that they name: `leaf_maps`: each leaf map is symmetric and positive definite. `leaf_nodes`: for each leaf and side, the entries are a permutation of 0 to 255.
All inputs are finite; a program needn't handle non-finite values.
Results may differ from a plain program's by a relative error of at most 0.0003.
Values sent between devices are 32-bit elements; how exact they have to be, the bound alone decides.
No kernel may reach another device: no remote copies, remote signals or barrier semaphores. Data moves between devices by JAX's collectives and lax.ppermute only.
A program may use at most 64 MiB of HBM per device.

v0:
```python
import jax
import jax.numpy as jnp
import numpy as np
from jax import lax
from jax.sharding import PartitionSpec as P

HALF_TABLE = ((0, 1, 1, 0), (0, 0, 1, 1), (1, 1, 0, 0), (1, 0, 0, 1))


def broadcast(block, axis, source):
    block = jnp.where(lax.axis_index(axis) == source, block, jnp.zeros_like(block))
    return lax.psum(block, axis)


def partner(value, axis, stride):
    return lax.ppermute(value, axis, [(i, i ^ 1 << stride) for i in range(lax.axis_size(axis))])


def cholesky_apply(factor, right_side):
    forward = lax.linalg.triangular_solve(factor, right_side, left_side=True, lower=True)
    return lax.linalg.triangular_solve(
        factor, forward, left_side=True, lower=True, transpose_a=True
    )


def highest_dot(left_matrix, right_matrix):
    return jnp.dot(
        left_matrix,
        right_matrix,
        precision=lax.Precision.HIGHEST,
        preferred_element_type=jnp.float32,
    )


def blocks(matrix, side_len, first_block, block_count):
    return matrix[first_block * side_len : (first_block + block_count) * side_len]


def shards(leaf_maps, leaf_nodes):
    side_len = leaf_maps.shape[2]
    leaf_panel = leaf_maps[0]
    side_nodes = leaf_nodes[0]
    box_place = lax.axis_index("box")
    column = lax.axis_index("col")
    sibling = box_place % 2
    pair_half = box_place // 2 % 2
    quarter = box_place % 4
    bases = (jnp.arange(4, dtype=jnp.int32) * side_len)[:, None]
    row_order = (bases + side_nodes).reshape(-1)
    own_nodes = jnp.take(side_nodes, column, axis=0)
    own_panel = jnp.take(jnp.take(leaf_panel, row_order, axis=0), own_nodes, axis=1)
    is_west = sibling == 0
    west_mask = is_west.astype(jnp.float32)
    east_mask = 1.0 - west_mask
    iface_own = broadcast(own_panel, "col", 1 + 2 * sibling)
    iface_peer = partner(iface_own, "box", 0)
    east_cols = jnp.where(is_west, iface_own, iface_peer)
    west_cols = jnp.where(is_west, iface_peer, iface_own)
    coupling = blocks(east_cols, side_len, 1, 1) + blocks(west_cols, side_len, 3, 1)
    coupling_rows = jnp.concatenate(
        [
            blocks(east_cols, side_len, 0, 1),
            blocks(west_cols, side_len, 0, 1),
            blocks(west_cols, side_len, 1, 1),
            blocks(east_cols, side_len, 2, 1),
            blocks(west_cols, side_len, 2, 1),
            blocks(east_cols, side_len, 3, 1),
        ],
        axis=0,
    )
    right_side = jnp.where(
        is_west, blocks(own_panel, side_len, 1, 1), blocks(own_panel, side_len, 3, 1)
    )
    diagonal_part = jnp.concatenate(
        [
            west_mask * blocks(own_panel, side_len, 0, 1),
            east_mask * blocks(own_panel, side_len, 0, 1),
            east_mask * blocks(own_panel, side_len, 1, 1),
            west_mask * blocks(own_panel, side_len, 2, 1),
            east_mask * blocks(own_panel, side_len, 2, 1),
            west_mask * blocks(own_panel, side_len, 3, 1),
        ],
        axis=0,
    )
    first_factor = jnp.linalg.cholesky(coupling)
    merged = diagonal_part - highest_dot(coupling_rows, cholesky_apply(first_factor, right_side))
    is_south = pair_half == 0
    root_col = jnp.where(is_south, 2, 0)
    half_own = broadcast(merged, "col", root_col)
    half_peer = partner(half_own, "box", 0)
    lower_half = jnp.where(is_west, half_own, half_peer)
    upper_half = jnp.where(is_west, half_peer, half_own)
    pair_stack = jnp.stack([lower_half, upper_half])
    other_stack = partner(pair_stack, "box", 1)
    own_pair = jnp.concatenate([pair_stack[0], pair_stack[1]], axis=1)
    other_pair = jnp.concatenate([other_stack[0], other_stack[1]], axis=1)
    north_cols = jnp.where(is_south, own_pair, other_pair)
    south_cols = jnp.where(is_south, other_pair, own_pair)
    coupling_two = blocks(north_cols, side_len, 3, 2) + blocks(south_cols, side_len, 0, 2)
    rows_two = jnp.concatenate(
        [
            blocks(north_cols, side_len, 0, 2),
            blocks(north_cols, side_len, 2, 1),
            blocks(south_cols, side_len, 2, 1),
            blocks(south_cols, side_len, 3, 2),
            blocks(north_cols, side_len, 5, 1),
            blocks(south_cols, side_len, 5, 1),
        ],
        axis=0,
    )
    second_factor = jnp.linalg.cholesky(coupling_two)
    holder = jnp.asarray(np.array(HALF_TABLE, dtype=np.int32))[quarter, column] == 0
    even_col = column % 2 == 0
    right_two = jnp.where(is_south, blocks(merged, side_len, 3, 2), blocks(merged, side_len, 0, 2))
    south_mask = is_south.astype(jnp.float32)
    north_mask = 1.0 - south_mask
    diag_two = jnp.concatenate(
        [
            south_mask * blocks(merged, side_len, 0, 2),
            south_mask * blocks(merged, side_len, 2, 1),
            north_mask * blocks(merged, side_len, 2, 1),
            north_mask * blocks(merged, side_len, 3, 2),
            south_mask * blocks(merged, side_len, 5, 1),
            north_mask * blocks(merged, side_len, 5, 1),
        ],
        axis=0,
    )
    solved, diag_two = (cholesky_apply(second_factor, right_two), diag_two)
    whole_panel = diag_two - highest_dot(rows_two, solved)
    top_rows = whole_panel[: 4 * side_len]
    bottom_rows = whole_panel[4 * side_len :]
    far_rows = partner(bottom_rows, "box", 1)
    near_rows = partner(bottom_rows, "box", 0)
    result = jnp.where(holder, top_rows, jnp.where(even_col, far_rows, near_rows))
    return result[None]


def solution(mesh):
    in_specs = (P("box", None, "col"), P("box", None, None))
    out_specs = P("box", None, "col")
    return jax.shard_map(shards, mesh=mesh, in_specs=in_specs, out_specs=out_specs, check_vma=False)
```

profile of v0, /device:TPU:2, one launch (start us, length us, event | category | flops | bytes accessed | tf_op | source)
XLA Modules:
  0.0 477.3 jit_solution(5407931225915577471)
XLA Ops:
  8.8 3.5 gather_fusion
  16.8 52.7 %all-reduce.5.cloned.1.call-done = f32[1024,256]{0,1:T(8,128)} async-done(((f32[1024,256]{0,1:T(8,128)}), f32[1024,256]{0,1:T(8,128)}) %all-reduce.5.cloned.1.call-update) | async-done | bytes 1048592 | tf_op jit(solution)/shard_map/psum | solution.py:12
  74.3 11.7 %cholesky.135 = f32[128,128]{1,0:T(8,128)S(1)} custom-call(f32[128,128]{1,0:T(8,128)S(1)} %copy.17), custom_call_target="Cholesky" | custom-call | tf_op jit(solution)/shard_map/jit(cholesky)/cholesky | solution.py:85
  86.1 9.8 %custom-call.46 = f32[1,128,128]{1,2,0:T(8,128)S(1)} custom-call(f32[1,128,128]{2,1,0:T(8,128)S(1)} %get-tuple-element.84), custom_call_target="InvertDiagBlocksLowerTriangular" | custom-call | tf_op jit(solution)/shard_map/jit(cholesky)/cholesky/custom-call.1 | solution.py:85
  98.2 11.7 %cholesky.145 = f32[128,128]{1,0:T(8,128)S(1)} custom-call(f32[128,128]{1,0:T(8,128)S(1)} %copy.20), custom_call_target="Cholesky" | custom-call | tf_op jit(solution)/shard_map/jit(cholesky)/cholesky | solution.py:85
  112.6 4.0 while.3
  116.6 19.7 %custom-call.41 = f32[2,128,128]{1,2,0:T(8,128)S(1)} custom-call(f32[2,128,128]{2,1,0:T(8,128)S(1)} %get-tuple-element.21), custom_call_target="InvertDiagBlocksLowerTriangular" | custom-call | tf_op jit(solution)/shard_map/triangular_solve | solution.py:21
  138.2 4.8 broadcast_select_fusion
  143.0 56.9 %all-reduce.7.cloned.1.call-done = f32[1536,256]{0,1:T(8,128)} async-done(((f32[1536,256]{0,1:T(8,128)}), f32[1536,256]{0,1:T(8,128)}) %all-reduce.7.cloned.1.call-update) | async-done | bytes 1572880 | tf_op jit(solution)/shard_map/psum | solution.py:12
  199.8 3.6 collective-permute-done.1
  213.7 64.3 %collective-permute-done.2 = f32[2,1536,256]{1,2,0:T(8,128)} collective-permute-done((f32[2,1536,256]{1,2,0:T(8,128)}, f32[2,1536,256]{1,2,0:T(8,128)}, u32[]{:S(2)}, u32[]{:S(2)}) %collective-permute-start.2) | collective-permute-done | bytes 3145760 | tf_op jit(solution)/shard_map/ppermute | solution.py:16
  278.0 2.1 slice_bitcast_fusion.1
  285.3 11.7 %cholesky.276 = f32[128,128]{1,0:T(8,128)S(1)} custom-call(f32[128,128]{1,0:T(8,128)S(1)} %cholesky.342), custom_call_target="Cholesky" | custom-call | tf_op jit(solution)/shard_map/jit(cholesky)/cholesky | solution.py:111
  297.1 2.8 slice.325
  304.1 9.8 %custom-call.42 = f32[1,128,128]{1,2,0:T(8,128)S(1)} custom-call(f32[1,128,128]{2,1,0:T(8,128)S(1)} %get-tuple-element.80), custom_call_target="InvertDiagBlocksLowerTriangular" | custom-call | tf_op jit(solution)/shard_map/jit(cholesky)/cholesky | solution.py:111
  314.6 11.9 %cholesky.294 = f32[128,128]{1,0:T(8,128)S(1)} custom-call(f32[128,128]{1,0:T(8,128)S(1)} %cholesky.346), custom_call_target="Cholesky" | custom-call | tf_op jit(solution)/shard_map/jit(cholesky)/cholesky | solution.py:111
  327.8 9.8 %custom-call.43 = f32[1,128,128]{1,2,0:T(8,128)S(1)} custom-call(f32[1,128,128]{2,1,0:T(8,128)S(1)} %get-tuple-element.77), custom_call_target="InvertDiagBlocksLowerTriangular" | custom-call | tf_op jit(solution)/shard_map/jit(cholesky)/cholesky | solution.py:111
  338.2 11.7 %cholesky.315 = f32[128,128]{1,0:T(8,128)S(1)} custom-call(f32[128,128]{1,0:T(8,128)S(1)} %cholesky.351), custom_call_target="Cholesky" | custom-call | tf_op jit(solution)/shard_map/jit(cholesky)/cholesky | solution.py:111
  350.6 9.8 %custom-call.47 = f32[1,128,128]{1,2,0:T(8,128)S(1)} custom-call(f32[1,128,128]{2,1,0:T(8,128)S(1)} %get-tuple-element.74), custom_call_target="InvertDiagBlocksLowerTriangular" | custom-call | tf_op jit(solution)/shard_map/jit(cholesky)/cholesky/custom-call.1 | solution.py:111
  361.0 11.7 %cholesky.328 = f32[128,128]{1,0:T(8,128)S(1)} custom-call(f32[128,128]{1,0:T(8,128)S(1)} %convolution_subtract_fusion.12), custom_call_target="Cholesky" | custom-call | tf_op jit(solution)/shard_map/jit(cholesky)/cholesky | solution.py:111
  376.1 10.4 %while.4 = (s32[]{:T(128)}, f32[512,512]{1,0:T(8,128)S(1)}, s32[4,2]{0,1:T(2,128)S(1)}, f32[4,128,128]{2,1,0:T(8,128)}, s32[]{:T(128)}) while((s32[]{:T(128)}, f32[512,512]{1,0:T(8,128)S(1)}, s32[4,2]{0,1:T(2,128)S(1)}, f32[4,128,128]{2,1,0:T(8,128)}, s32[]{:T(128)}) %tuple.64), condition=%wide.while_cond.2, body=%wide.while_body.2.sunk | while | flops 2 | bytes 132705 | solution.py:21
  386.5 40.1 %custom-call.44 = f32[4,128,128]{1,2,0:T(8,128)S(1)} custom-call(f32[4,128,128]{2,1,0:T(8,128)} %get-tuple-element.29), custom_call_target="InvertDiagBlocksLowerTriangular" | custom-call | tf_op jit(solution)/shard_map/triangular_solve | solution.py:21
  433.9 5.6 %fusion.8 = f32[2048,256]{0,1:T(8,128)S(1)} fusion(f32[2048,256]{0,1:T(8,128)} %copy-done.18, f32[256,512]{0,1:T(8,128)S(1)} %copy-done.17, f32[256,512]{0,1:T(8,128)S(1)} %copy-done.16, f32[768,512]{0,1:T(8,128)S(1)} %copy-done.12, f32[768,512]{0,1:T(8,128)S(1)} %copy-done.11, f32[128,256]{1,0:T(8,128)S(1)} %fusion.78, f32[128,256]{1,0:T(8,128)S(1)} %fusion.76, ...), kind=kOutput, calls=%fused_computation.18 | convolution fusion | flops 3225288704 | bytes 8912896 | tf_op jit(solution)/shard_map/dot_general | solution.py:27
  445.4 21.1 %collective-permute-done.3 = f32[1024,256]{0,1:T(8,128)S(1)} collective-permute-done((f32[1024,256]{0,1:T(8,128)}, f32[1024,256]{0,1:T(8,128)S(1)}, u32[]{:S(2)}, u32[]{:S(2)}) %collective-permute-start.3) | collective-permute-done | bytes 1048608 | tf_op jit(solution)/shard_map/ppermute | solution.py:16
  (171 shorter events, 71.3 us)
Async XLA Ops:
  6.5 2.3 copy-start
  6.5 63.0 %all-reduce.5.cloned.1.call-start = ((), (), s32[]{:S(2)}) async-start(), calls=%async_computation | async-start | bytes 2097152 | tf_op jit(solution)/shard_map/psum | solution.py:12
  15.1 184.7 %all-reduce.7.cloned.1.call-start = ((), (), s32[]{:S(2)}) async-start(), calls=%async_computation.1 | async-start | bytes 3145728 | tf_op jit(solution)/shard_map/psum | solution.py:12
  69.5 3.3 copy-start.13
  69.5 3.3 collective-permute-start
  199.8 3.6 collective-permute-start.1
  205.1 2.1 copy-start.1
  207.2 70.8 %collective-permute-start.2 = (f32[2,1536,256]{1,2,0:T(8,128)}, f32[2,1536,256]{1,2,0:T(8,128)}, u32[]{:S(2)}, u32[]{:S(2)}) collective-permute-start(f32[2,1536,256]{1,2,0:T(8,128)} %pad_maximum_fusion.1), channel_id=1, source_target_pairs={{0,8},{4,12},{8,0},{12,4},{16,24},{20,28},{24,16},{28,20},{32,40},... | collective-permute-start | bytes 9437192 | tf_op jit(solution)/shard_map/ppermute | solution.py:16
  209.1 2.2 copy-start.6
  212.4 1.3 copy-start.18
  213.7 66.4 %copy-start.2 = (f32[1536,256]{0,1:T(8,128)S(1)}, f32[1536,256]{0,1:T(8,128)}, u32[]{:S(2)}) copy-start(f32[1536,256]{0,1:T(8,128)} %copy-done.1) | copy-start | bytes 4718596
  281.0 1.7 copy-start.3
  281.0 2.6 copy-start.5
  284.3 1.0 copy-start.7
  297.1 2.9 copy-start.4
  301.2 12.7 %copy-start.8 = (f32[512,512]{1,0:T(8,128)S(1)}, f32[512,512]{1,0:T(8,128)}, u32[]{:S(2)}) copy-start(f32[512,512]{1,0:T(8,128)} %copy-done.7) | copy-start | bytes 3145732
  376.1 53.4 %copy-start.10 = (f32[512,256]{0,1:T(8,128)S(1)}, f32[512,256]{0,1:T(8,128)}, u32[]{:S(2)}) copy-start(f32[512,256]{0,1:T(8,128)} %get-tuple-element.65) | copy-start | bytes 1572868
  430.4 3.5 copy-start.16
  430.4 3.5 copy-start.17
  431.5 2.4 copy-start.11
  431.5 2.4 copy-start.12
  439.5 1.3 copy-start.9
  441.9 24.6 %collective-permute-start.3 = (f32[1024,256]{0,1:T(8,128)}, f32[1024,256]{0,1:T(8,128)S(1)}, u32[]{:S(2)}, u32[]{:S(2)}) collective-permute-start(f32[1024,256]{0,1:T(8,128)} %slice.332), channel_id=1, source_target_pairs={{0,8},{4,12},{8,0},{12,4},{16,24},{20,28},{24,16},{28,20},{32,40},... | collective-permute-start | bytes 3145736 | tf_op jit(solution)/shard_map/ppermute | solution.py:16
  443.4 23.0 %collective-permute-start.4 = (f32[1024,256]{0,1:T(8,128)}, f32[1024,256]{0,1:T(8,128)S(1)}, u32[]{:S(2)}, u32[]{:S(2)}) collective-permute-start(f32[1024,256]{0,1:T(8,128)} %slice.332), channel_id=1, source_target_pairs={{0,4},{4,0},{8,12},{12,8},{16,20},{20,16},{24,28},{28,24},{32,36},... | collective-permute-start | bytes 3145736 | tf_op jit(solution)/shard_map/ppermute | solution.py:16
  (2 other events, 1.7 us)
Sparse Core Ops, SparseCore 0:
  15.3 54.2 all-reduce.4
  143.1 56.6 all-reduce.6
where the time goes:
time: 480 us; the launch traced here: 477 us
  waiting for transfers between devices  199 us (41%)
  other arithmetic  190 us (40%)
  local copies, waits for them, and re-layouts  41.9 us (9%)
  matrix products  23.4 us (5%)
  between operations  18.7 us (4%)
    psum x2, waiting for transfers between devices, broadcast(): return lax.psum(block, axis)  110 us
    ppermute x5, waiting for transfers between devices, partner(): lax.ppermute(value, axis, [(i, i ^ 1 << stride) for i in range(lax.axis_s...  89 us
    another operation x15, other arithmetic, shards(): second_factor = jnp.linalg.cholesky(coupling_two)  79.2 us
    another operation x6, other arithmetic, cholesky_apply(): lax.linalg.triangular_solve(factor, forward, left_side=True, lower=True,...  60 us
    another operation x7, other arithmetic, shards(): first_factor = jnp.linalg.cholesky(coupling)  34.6 us
    another operation x18, local copies, waits for them, and re-layouts  13.9 us
    dot_general x2, matrix products, highest_dot(): jnp.dot(left_matrix, right_matrix, precision=lax.Precision.HIGHEST, prefe...  10.3 us
    unnamed x47, local copies, waits for them, and re-layouts  9.61 us
  transfers between devices with their start and end apart: 7, of which 5 were waited for; matrix products, arithmetic and copies ran while one was open for 2% of the time, Pallas kernels for 0%

commit v1 on v0

--- a/solution.py
+++ b/solution.py
@@ -9,7 +9,7 @@
 
 def broadcast(block, axis, source):
     block = jnp.where(lax.axis_index(axis) == source, block, jnp.zeros_like(block))
-    return lax.psum(block, axis)
+    return jnp.sum(lax.all_gather(block, axis), axis=0)
 
 
 def partner(value, axis, stride):

time: 480 us -> 504 us (1.050)
  other arithmetic: 190 us -> 202 us
  waiting for transfers between devices: 199 us -> 209 us
    all_gather x0 -> x2, waiting for transfers between devices: none -> 121 us  [broadcast(): return jnp.sum(lax.all_gather(block, axis), axis=0)]
    psum x2 -> x0, waiting for transfers between devices: 110 us -> none  [broadcast(): return lax.psum(block, axis)]
    reduce_sum x0 -> x2, other arithmetic: none -> 5.99 us  [broadcast(): return jnp.sum(lax.all_gather(block, axis), axis=0)]
    another operation x6, matrix products: 1.87 us -> 7.76 us  [shards(): second_factor = jnp.linalg.cholesky(coupling_two)]
where the time goes in v1:
time: 504 us; the launch traced here: 500 us
  waiting for transfers between devices  209 us (41%)
  other arithmetic  202 us (40%)
  local copies, waits for them, and re-layouts  38.5 us (8%)
  matrix products  27.2 us (5%)
  between operations  18.9 us (4%)
    all_gather x2, waiting for transfers between devices, broadcast(): return jnp.sum(lax.all_gather(block, axis), axis=0)  121 us
    ppermute x5, waiting for transfers between devices, partner(): lax.ppermute(value, axis, [(i, i ^ 1 << stride) for i in range(lax.axis_s...  87.7 us
    another operation x15, other arithmetic, shards(): second_factor = jnp.linalg.cholesky(coupling_two)  81.2 us
    another operation x6, other arithmetic, cholesky_apply(): lax.linalg.triangular_solve(factor, forward, left_side=True, lower=True,...  60.4 us
    another operation x7, other arithmetic, shards(): first_factor = jnp.linalg.cholesky(coupling)  34.6 us
    dot_general x2, matrix products, highest_dot(): jnp.dot(left_matrix, right_matrix, precision=lax.Precision.HIGHEST, prefe...  12.9 us
    another operation x18, local copies, waits for them, and re-layouts  12 us
  transfers between devices with their start and end apart: 7, of which 5 were waited for; matrix products, arithmetic and copies ran while one was open for 2% of the time, Pallas kernels for 0%

profile of v1, /device:TPU:2, one launch (start us, length us, event | category | flops | bytes accessed | tf_op | source)
XLA Modules:
  0.0 499.8 jit_solution(8555787549502818260)
XLA Ops:
  8.8 3.5 gather_fusion
  17.1 52.2 %all-gather.4.cloned.1.call-done = f32[4,1024,256]{2,1,0:T(8,128)} async-done(((f32[1,1024,256]{2,1,0:T(8,128)}), f32[4,1024,256]{2,1,0:T(8,128)}) %all-gather.4.cloned.1.call-update) | async-done | bytes 4194320 | tf_op jit(solution)/shard_map/all_gather | solution.py:12
  69.3 2.6 reduce_sum.18
  76.1 11.7 %cholesky.135 = f32[128,128]{1,0:T(8,128)S(1)} custom-call(f32[128,128]{1,0:T(8,128)S(1)} %cholesky.339), custom_call_target="Cholesky" | custom-call | tf_op jit(solution)/shard_map/jit(cholesky)/cholesky | solution.py:85
  87.8 9.8 %custom-call.46 = f32[1,128,128]{1,2,0:T(8,128)S(1)} custom-call(f32[1,128,128]{2,1,0:T(8,128)S(1)} %get-tuple-element.82), custom_call_target="InvertDiagBlocksLowerTriangular" | custom-call | tf_op jit(solution)/shard_map/jit(cholesky)/cholesky/custom-call.1 | solution.py:85
  98.1 11.7 %cholesky.145 = f32[128,128]{1,0:T(8,128)S(1)} custom-call(f32[128,128]{1,0:T(8,128)S(1)} %convolution_subtract_fusion.11), custom_call_target="Cholesky" | custom-call | tf_op jit(solution)/shard_map/jit(cholesky)/cholesky | solution.py:85
  112.7 4.3 while.3
  116.9 19.7 %custom-call.41 = f32[2,128,128]{1,2,0:T(8,128)S(1)} custom-call(f32[2,128,128]{2,1,0:T(8,128)S(1)} %get-tuple-element.21), custom_call_target="InvertDiagBlocksLowerTriangular" | custom-call | tf_op jit(solution)/shard_map/triangular_solve | solution.py:21
  138.4 5.8 %broadcast_select_fusion = (f32[1536,256]{1,0:T(8,128)}, f32[1536,256]{1,0:T(8,128)}) fusion(pred[]{:T(512)S(6)} %eq.31, f32[1536,256]{1,0:T(8,128)} %multiply_dynamic-update-slice_fusion.6, f32[1536,256]{0,1:T(8,128)S(1)} %get-tuple-element.66, f32[128,256]{1,0:T(8,128)S(1)} %fusion.72, f32[128,256]{1,0:T(8,128)S(1)} %fusion.71), kind=kOutput, calls=%fused_computation.49 | convolution fusion | flops 1208811520 | bytes 6553601 | tf_op jit(solution)/shard_map/dot_general | solution.py:27
  144.2 68.8 %all-gather.6.cloned.1.call-done = f32[6144,256]{1,0:T(8,128)} async-done(((f32[1536,256]{1,0:T(8,128)}), f32[6144,256]{1,0:T(8,128)}) %all-gather.6.cloned.1.call-update) | async-done | bytes 6291472 | tf_op jit(solution)/shard_map/all_gather | solution.py:12
  213.0 3.4 reduce_sum.19
  230.4 64.4 %collective-permute-done.2 = f32[2,1536,256]{1,2,0:T(8,128)} collective-permute-done((f32[2,1536,256]{1,2,0:T(8,128)}, f32[2,1536,256]{1,2,0:T(8,128)}, u32[]{:S(2)}, u32[]{:S(2)}) %collective-permute-start.2) | collective-permute-done | bytes 3145760 | tf_op jit(solution)/shard_map/ppermute | solution.py:16
  301.5 2.6 copy.26
  307.1 11.7 %cholesky.276 = f32[128,128]{1,0:T(8,128)S(1)} custom-call(f32[128,128]{1,0:T(8,128)S(1)} %cholesky.342), custom_call_target="Cholesky" | custom-call | tf_op jit(solution)/shard_map/jit(cholesky)/cholesky | solution.py:111
  325.3 9.8 %custom-call.42 = f32[1,128,128]{1,2,0:T(8,128)S(1)} custom-call(f32[1,128,128]{2,1,0:T(8,128)S(1)} %get-tuple-element.78), custom_call_target="InvertDiagBlocksLowerTriangular" | custom-call | tf_op jit(solution)/shard_map/jit(cholesky)/cholesky | solution.py:111
  338.3 11.8 %cholesky.294 = f32[128,128]{1,0:T(8,128)S(1)} custom-call(f32[128,128]{1,0:T(8,128)S(1)} %cholesky.346), custom_call_target="Cholesky" | custom-call | tf_op jit(solution)/shard_map/jit(cholesky)/cholesky | solution.py:111
  352.1 9.8 %custom-call.43 = f32[1,128,128]{1,2,0:T(8,128)S(1)} custom-call(f32[1,128,128]{2,1,0:T(8,128)S(1)} %get-tuple-element.75), custom_call_target="InvertDiagBlocksLowerTriangular" | custom-call | tf_op jit(solution)/shard_map/jit(cholesky)/cholesky | solution.py:111
  364.3 11.7 %cholesky.315 = f32[128,128]{1,0:T(8,128)S(1)} custom-call(f32[128,128]{1,0:T(8,128)S(1)} %cholesky.351), custom_call_target="Cholesky" | custom-call | tf_op jit(solution)/shard_map/jit(cholesky)/cholesky | solution.py:111
  377.3 9.8 %custom-call.47 = f32[1,128,128]{1,2,0:T(8,128)S(1)} custom-call(f32[1,128,128]{2,1,0:T(8,128)S(1)} %get-tuple-element.72), custom_call_target="InvertDiagBlocksLowerTriangular" | custom-call | tf_op jit(solution)/shard_map/jit(cholesky)/cholesky/custom-call.1 | solution.py:111
  389.4 11.9 %cholesky.328 = f32[128,128]{1,0:T(8,128)S(1)} custom-call(f32[128,128]{1,0:T(8,128)S(1)} %convolution_subtract_fusion.12), custom_call_target="Cholesky" | custom-call | tf_op jit(solution)/shard_map/jit(cholesky)/cholesky | solution.py:111
  406.5 8.1 %while.4 = (s32[]{:T(128)}, f32[512,512]{1,0:T(8,128)S(1)}, s32[4,2]{0,1:T(2,128)S(1)}, f32[4,128,128]{2,1,0:T(8,128)S(1)}, s32[]{:T(128)}) while((s32[]{:T(128)}, f32[512,512]{1,0:T(8,128)S(1)}, s32[4,2]{0,1:T(2,128)S(1)}, f32[4,128,128]{2,1,0:T(8,128)S(1)}, s32[]{:T(128)}) %tuple.63), condition=%wide.while_cond.2, body=%wide.while_body.2.sunk | while | flops 2 | bytes 131181 | solution.py:21
  414.6 39.3 %custom-call.44 = f32[4,128,128]{1,2,0:T(8,128)S(1)} custom-call(f32[4,128,128]{2,1,0:T(8,128)S(1)} %get-tuple-element.29), custom_call_target="InvertDiagBlocksLowerTriangular" | custom-call | tf_op jit(solution)/shard_map/triangular_solve | solution.py:21
  458.5 7.1 %fusion.8 = f32[2048,256]{1,0:T(8,128)S(1)} fusion(f32[2048,256]{1,0:T(8,128)S(1)} %copy-done.15, f32[256,512]{0,1:T(8,128)S(1)} %copy-done.13, f32[256,512]{0,1:T(8,128)S(1)} %copy-done.12, f32[768,512]{0,1:T(8,128)S(1)} %copy-done.11, f32[768,512]{0,1:T(8,128)S(1)} %copy-done.10, f32[128,256]{1,0:T(8,128)S(1)} %fusion.79, f32[128,256]{1,0:T(8,128)S(1)} %fusion.77, ...), kind=kOutput, calls=%fused_computation.18 | convolution fusion | flops 3225288704 | bytes 8912896 | tf_op jit(solution)/shard_map/dot_general | solution.py:27
  469.3 21.0 %collective-permute-done.3 = f32[1024,256]{1,0:T(8,128)} collective-permute-done((f32[1024,256]{1,0:T(8,128)S(1)}, f32[1024,256]{1,0:T(8,128)}, u32[]{:S(2)}, u32[]{:S(2)}) %collective-permute-start.3) | collective-permute-done | bytes 1048608 | tf_op jit(solution)/shard_map/ppermute | solution.py:16
  (168 shorter events, 80.4 us)
Async XLA Ops:
  6.5 2.3 copy-start
  6.5 62.7 %all-gather.4.cloned.1.call-start = ((), (), s32[]{:S(2)}) async-start(), calls=%async_computation | async-start | bytes 5242880 | tf_op jit(solution)/shard_map/all_gather | solution.py:12
  15.4 197.6 %all-gather.6.cloned.1.call-start = ((), (), s32[]{:S(2)}) async-start(), calls=%async_computation.1 | async-start | bytes 7864320 | tf_op jit(solution)/shard_map/all_gather | solution.py:12
  72.2 3.2 collective-permute-start
  216.9 1.1 copy-start.7
  216.9 3.5 collective-permute-start.1
  223.9 70.8 %collective-permute-start.2 = (f32[2,1536,256]{1,2,0:T(8,128)}, f32[2,1536,256]{1,2,0:T(8,128)}, u32[]{:S(2)}, u32[]{:S(2)}) collective-permute-start(f32[2,1536,256]{1,2,0:T(8,128)} %pad_maximum_fusion.1), channel_id=1, source_target_pairs={{0,8},{4,12},{8,0},{12,4},{16,24},{20,28},{24,16},{28,20},{32,40},... | collective-permute-start | bytes 9437192 | tf_op jit(solution)/shard_map/ppermute | solution.py:16
  225.9 2.2 copy-start.6
  229.0 1.4 copy-start.14
  297.7 1.6 copy-start.2
  297.7 2.7 copy-start.4
  304.1 15.9 %copy-start.5 = (f32[1536,512]{0,1:T(8,128)S(1)}, f32[1536,512]{0,1:T(8,128)}, u32[]{:S(2)}) copy-start(f32[1536,512]{0,1:T(8,128)} %copy-done.4) | copy-start | bytes 9437188
  306.0 1.1 copy-start.8
  319.9 2.5 copy-start.3
  389.4 64.5 %copy-start.9 = (f32[512,256]{1,0:T(8,128)S(1)}, f32[512,256]{1,0:T(8,128)}, u32[]{:S(2)}) copy-start(f32[512,256]{1,0:T(8,128)} %get-tuple-element.63) | copy-start | bytes 1572868
  453.9 4.6 copy-start.15
  455.4 3.1 copy-start.12
  455.4 3.1 copy-start.13
  456.2 2.4 copy-start.10
  456.2 2.4 copy-start.11
  465.7 24.6 %collective-permute-start.3 = (f32[1024,256]{1,0:T(8,128)S(1)}, f32[1024,256]{1,0:T(8,128)}, u32[]{:S(2)}, u32[]{:S(2)}) collective-permute-start(f32[1024,256]{1,0:T(8,128)S(1)} %slice.332), channel_id=1, source_target_pairs={{0,8},{4,12},{8,0},{12,4},{16,24},{20,28},{24,16},{28,20},{32,40},... | collective-permute-start | bytes 3145736 | tf_op jit(solution)/shard_map/ppermute | solution.py:16
  467.4 22.9 %collective-permute-start.4 = (f32[1024,256]{1,0:T(8,128)S(1)}, f32[1024,256]{1,0:T(8,128)}, u32[]{:S(2)}, u32[]{:S(2)}) collective-permute-start(f32[1024,256]{1,0:T(8,128)S(1)} %slice.332), channel_id=1, source_target_pairs={{0,4},{4,0},{8,12},{12,8},{16,20},{20,16},{24,28},{28,24},{32,36},... | collective-permute-start | bytes 3145736 | tf_op jit(solution)/shard_map/ppermute | solution.py:16
  490.3 2.5 copy-start.1
Sparse Core Ops, SparseCore 0:
  15.5 53.7 all-gather.3
  144.3 68.6 all-gather.5
